TPU v7x, 32 devices: a whole 2x2x4 slice. The times are simulated.
32 devices in a mesh: rep: 4 (over y, core), shard: 8 (over z, x).
Axes of the slice: x: 2, y: 2, z: 4, core: 2. Of those that a mesh axis runs over, the one named last changes fastest.
Arguments:
- tokens: bfloat16 [32, 512, 1152], P(('rep', 'shard')), may hold values from -6 to 6
- cotangent: bfloat16 [32, 512, 1152], P(('rep', 'shard')), may hold values from -6 to 6
- adapter_ids: int32 [32, 1], P(('rep', 'shard')), may hold values from 0 to 7
- gain_one: float32 [1152], replicated, may hold values from 0.5 to 1.5
- shift_one: float32 [1152], replicated, may hold values from -1.5 to 1.5
- gain_two: float32 [1152], replicated, may hold values from 0.5 to 1.5
- shift_two: float32 [1152], replicated, may hold values from -1.5 to 1.5
- qkv_weight: bfloat16 [3, 1152, 1152], P(None, 'shard'), may hold values from -0.1875 to 0.1875
- out_weight: bfloat16 [1152, 1152], P('shard'), may hold values from -0.5 to 0.5
- mlp_first: bfloat16 [1152, 4304], P('shard'), may hold values from -0.1875 to 0.1875
- mlp_second: bfloat16 [4304, 1152], P(None, 'shard'), may hold values from -0.09375 to 0.09375
- down_narrow: bfloat16 [5, 128, 1152], P(None, 'shard'), may hold values from -0.1875 to 0.1875
- down_wide: bfloat16 [128, 4304], P('shard'), may hold values from -0.09375 to 0.09375
- up_narrow: bfloat16 [5, 128, 1152], P(None, 'shard'), may hold values from -1.5 to 1.5
- up_wide: bfloat16 [128, 4304], P('shard'), may hold values from -1.5 to 1.5
Outputs:
- output: bfloat16 [32, 512, 1152], P(('rep', 'shard'))
- input_grad: bfloat16 [32, 512, 1152], P(('rep', 'shard'))
- grad_down_narrow: float32 [5, 128, 1152], P(None, 'shard')
- grad_down_wide: float32 [128, 4304], P('shard')
- grad_up_narrow: float32 [5, 128, 1152], P(None, 'shard')
- grad_up_wide: float32 [128, 4304], P('shard')
Inputs may be any that keep to these rules, and one draw needn't show every extreme that they name: `adapter_ids`: every adapter is used by some image.
All inputs are finite; a program needn't handle non-finite values.
Results may differ from a plain program's by a relative error of at most 0.019.
The roundings to bfloat16 on the way count: a program that leaves them out, or rounds other values in their place, can miss the bound.
Values may be sent and summed in bfloat16 or wider, within the bound.
A program may use at most 256 MiB of HBM per device.

v0:
```python
import jax
import jax.numpy as jnp
from jax import lax
from jax.sharding import PartitionSpec as P

HEAD_DIM = 72
RANK = 16


GELU_SCALE = 0.7978845608028654
GELU_CUBE = 0.044715


def dot_plain(left, right):
    return jnp.dot(left, right, preferred_element_type=jnp.float32)


def dot_last(left, right):
    return lax.dot_general(
        left, right, (((1,), (1,)), ((), ())), preferred_element_type=jnp.float32
    )


def dot_first(left, right):
    return lax.dot_general(
        left, right, (((0,), (0,)), ((), ())), preferred_element_type=jnp.float32
    )


def layer_stats(value):
    average = jnp.mean(value, axis=-1, keepdims=True)
    centred = value - average
    spread = jnp.mean(centred * centred, axis=-1, keepdims=True)
    inverse = lax.rsqrt(spread + 1e-06)
    return (centred * inverse, inverse)


def norm_back(gradient, normal_part, inverse, gain):
    scaled = gradient * gain
    return inverse * (
        scaled
        - jnp.mean(scaled, axis=-1, keepdims=True)
        - normal_part * jnp.mean(scaled * normal_part, axis=-1, keepdims=True)
    )


def gelu_slope(value):
    tangent = jnp.tanh(GELU_SCALE * (value + GELU_CUBE * value * value * value))
    return 0.5 * (1.0 + tangent) + 0.5 * value * (1.0 - tangent * tangent) * GELU_SCALE * (
        1.0 + 3.0 * GELU_CUBE * value * value
    )


def adapter_in(inputs, down, select):
    return (dot_last(inputs, down) * select).astype(jnp.bfloat16)


def adapter_back(grad_out, inputs, inner, down, up, select):
    grad_inner = dot_last(grad_out, up).astype(jnp.bfloat16) * select.astype(jnp.bfloat16)
    return (dot_plain(grad_inner, down), dot_first(grad_inner, inputs), dot_first(inner, grad_out))


def split_heads(value, heads):
    return value.reshape(value.shape[0], heads, value.shape[1] // heads)


def per_device(
    tokens,
    cotangent,
    adapter_ids,
    gain_one,
    shift_one,
    gain_two,
    shift_two,
    qkv_weight,
    out_weight,
    mlp_first,
    mlp_second,
    down_narrow,
    down_wide,
    up_narrow,
    up_wide,
):
    hidden_in = tokens[0].astype(jnp.float32)
    seq_len, width = hidden_in.shape
    heads = width // HEAD_DIM
    scaling = HEAD_DIM ** (-0.5)
    narrow_down, wide_down, narrow_up, wide_up = (
        lax.all_gather(down_narrow, "shard", axis=1, tiled=True),
        lax.all_gather(down_wide, "shard", axis=0, tiled=True),
        lax.all_gather(up_narrow, "shard", axis=1, tiled=True),
        lax.all_gather(up_wide, "shard", axis=0, tiled=True),
    )
    ranks = narrow_down.shape[1]
    select = (lax.broadcasted_iota(jnp.int32, (1, ranks), 1) // RANK == adapter_ids[0, 0]).astype(
        jnp.float32
    )
    normal_one, inverse_one = layer_stats(hidden_in)
    normed = (normal_one * gain_one + shift_one).astype(jnp.bfloat16)
    columns = normed
    qkv_main = jnp.einsum(
        "tr,jre->jte",
        columns,
        lax.all_gather(qkv_weight, "shard", axis=1, tiled=True),
        preferred_element_type=jnp.float32,
    )
    inner_qkv = [adapter_in(normed, narrow_down[member], select) for member in range(3)]
    projected = [
        (qkv_main[member] + dot_plain(inner_qkv[member], narrow_up[member])).astype(jnp.bfloat16)
        for member in range(3)
    ]
    query_heads = split_heads(projected[0], heads)
    key_heads = split_heads(projected[1], heads)
    value_heads = split_heads(projected[2], heads)
    scores = (
        jnp.einsum("qhd,khd->hqk", query_heads, key_heads, preferred_element_type=jnp.float32)
        * scaling
    )
    row_top = jnp.max(scores, axis=-1, keepdims=True)
    exponent = jnp.exp(scores - row_top)
    row_total = jnp.sum(exponent, axis=-1, keepdims=True)
    log_total = row_top + jnp.log(row_total)
    probs_low = (exponent / row_total).astype(jnp.bfloat16)
    attended = jnp.einsum(
        "hqk,khd->qhd", probs_low, value_heads, preferred_element_type=jnp.float32
    )
    attended = attended.reshape(seq_len, width).astype(jnp.bfloat16)
    columns = attended
    out_main = dot_plain(columns, lax.all_gather(out_weight, "shard", axis=0, tiled=True))
    inner_out = adapter_in(attended, narrow_down[3], select)
    middle = hidden_in + (out_main + dot_plain(inner_out, narrow_up[3]))
    normal_two, inverse_two = layer_stats(middle)
    normed_two = (normal_two * gain_two + shift_two).astype(jnp.bfloat16)
    columns = normed_two
    first_main = dot_plain(columns, lax.all_gather(mlp_first, "shard", axis=0, tiled=True))
    inner_one = adapter_in(normed_two, narrow_down[4], select)
    before = first_main + dot_plain(inner_one, wide_up)
    active = jax.nn.gelu(before, approximate=True).astype(jnp.bfloat16)
    second_main = dot_plain(active, lax.all_gather(mlp_second, "shard", axis=1, tiled=True))
    inner_two = adapter_in(active, wide_down, select)
    output = (middle + (second_main + dot_plain(inner_two, narrow_up[4]))).astype(jnp.bfloat16)
    grad_after = cotangent[0]
    columns = grad_after
    active_main = dot_last(columns, lax.all_gather(mlp_second, "shard", axis=1, tiled=True))
    back_two, grad_wide_down, grad_up_fc = adapter_back(
        grad_after, active, inner_two, wide_down, narrow_up[4], select
    )
    grad_before = ((active_main + back_two) * gelu_slope(before)).astype(jnp.bfloat16)
    normed_two_main = dot_last(grad_before, lax.all_gather(mlp_first, "shard", axis=0, tiled=True))
    back_one, grad_down_fc, grad_wide_up = adapter_back(
        grad_before, normed_two, inner_one, narrow_down[4], wide_up, select
    )
    grad_middle = cotangent[0].astype(jnp.float32) + norm_back(
        normed_two_main + back_one, normal_two, inverse_two, gain_two
    )
    grad_branch = grad_middle.astype(jnp.bfloat16)
    attended_main = dot_last(grad_branch, lax.all_gather(out_weight, "shard", axis=0, tiled=True))
    back_out, grad_down_out, grad_up_out = adapter_back(
        grad_branch, attended, inner_out, narrow_down[3], narrow_up[3], select
    )
    grad_attended = split_heads((attended_main + back_out).astype(jnp.bfloat16), heads)
    again_scores = (
        jnp.einsum("qhd,khd->hqk", query_heads, key_heads, preferred_element_type=jnp.float32)
        * scaling
    )
    probs_again = jnp.exp(again_scores - log_total)
    grad_probs = jnp.einsum(
        "qhd,khd->hqk", grad_attended, value_heads, preferred_element_type=jnp.float32
    )
    grad_value = jnp.einsum(
        "hqk,qhd->khd",
        probs_again.astype(jnp.bfloat16),
        grad_attended,
        preferred_element_type=jnp.float32,
    )
    grad_scores = probs_again * (
        grad_probs - jnp.sum(grad_probs * probs_again, axis=-1, keepdims=True)
    )
    grad_scores = grad_scores.astype(jnp.bfloat16)
    grad_query = (
        jnp.einsum("hqk,khd->qhd", grad_scores, key_heads, preferred_element_type=jnp.float32)
        * scaling
    )
    grad_key = (
        jnp.einsum("hqk,qhd->khd", grad_scores, query_heads, preferred_element_type=jnp.float32)
        * scaling
    )
    grad_qkv = jnp.stack(
        [
            grad_query.reshape(seq_len, width),
            grad_key.reshape(seq_len, width),
            grad_value.reshape(seq_len, width),
        ]
    ).astype(jnp.bfloat16)
    normed_main = jnp.einsum(
        "jte,jre->tr",
        grad_qkv,
        lax.all_gather(qkv_weight, "shard", axis=1, tiled=True),
        preferred_element_type=jnp.float32,
    )
    grad_downs = []
    grad_ups = []
    for member in range(3):
        back_member, grad_down_member, grad_up_member = adapter_back(
            grad_qkv[member],
            normed,
            inner_qkv[member],
            narrow_down[member],
            narrow_up[member],
            select,
        )
        normed_main = normed_main + back_member
        grad_downs.append(grad_down_member)
        grad_ups.append(grad_up_member)
    input_grad = (grad_middle + norm_back(normed_main, normal_one, inverse_one, gain_one)).astype(
        jnp.bfloat16
    )
    local_down_narrow = jnp.stack(grad_downs + [grad_down_out, grad_down_fc])
    local_up_narrow = jnp.stack(grad_ups + [grad_up_out, grad_up_fc])
    shares = (
        lax.psum_scatter(local_down_narrow, "shard", scatter_dimension=1, tiled=True),
        lax.psum_scatter(grad_wide_down, "shard", scatter_dimension=0, tiled=True),
        lax.psum_scatter(local_up_narrow, "shard", scatter_dimension=1, tiled=True),
        lax.psum_scatter(grad_wide_up, "shard", scatter_dimension=0, tiled=True),
    )
    totals = (
        lax.psum(shares[0].astype(jnp.bfloat16), "rep").astype(jnp.float32),
        lax.psum(shares[1].astype(jnp.bfloat16), "rep").astype(jnp.float32),
        lax.psum(shares[2].astype(jnp.bfloat16), "rep").astype(jnp.float32),
        lax.psum(shares[3].astype(jnp.bfloat16), "rep").astype(jnp.float32),
    )
    return (output[None], input_grad[None], totals[0], totals[1], totals[2], totals[3])


def solution(mesh):
    return jax.shard_map(
        per_device,
        mesh=mesh,
        in_specs=(
            P(("rep", "shard"), None, None),
            P(("rep", "shard"), None, None),
            P(("rep", "shard"), None),
            P(),
            P(),
            P(),
            P(),
            P(None, "shard", None),
            P("shard", None),
            P("shard", None),
            P(None, "shard"),
            P(None, "shard", None),
            P("shard", None),
            P(None, "shard", None),
            P("shard", None),
        ),
        out_specs=(
            P(("rep", "shard"), None, None),
            P(("rep", "shard"), None, None),
            P(None, "shard", None),
            P("shard", None),
            P(None, "shard", None),
            P("shard", None),
        ),
        check_vma=False,
    )
```

profile of v0, /device:TPU:0, one launch (start us, length us, event | category | flops | bytes accessed | tf_op | source)
XLA Modules:
  0.0 992.5 jit_solution(835571023374945255)
XLA Ops:
  15.7 40.8 %all-gather.11.cloned.1.call-done = bf16[5,128,1152]{2,1,0:T(8,128)(2,1)} async-done(((bf16[5,16,1152]{2,1,0:T(8,128)(2,1)}), bf16[5,128,1152]{2,1,0:T(8,128)(2,1)}) %all-gather.11.cloned.1.call-update) | async-done | bytes 1474576 | tf_op jit(solution)/shard_map/all_gather | solution.py:89
  56.5 2.1 fusion.81
  62.7 38.0 %all-gather.13.cloned.1.call-done = bf16[5,128,1152]{2,1,0:T(8,128)(2,1)} async-done(((bf16[5,16,1152]{2,1,0:T(8,128)(2,1)}), bf16[5,128,1152]{2,1,0:T(8,128)(2,1)}) %all-gather.13.cloned.1.call-update) | async-done | bytes 1474576 | tf_op jit(solution)/shard_map/all_gather | solution.py:91
  102.8 118.3 %all-gather.9.cloned.1.call-done = bf16[3,1152,1152]{2,1,0:T(8,128)(2,1)} async-done(((bf16[3,144,1152]{2,1,0:T(8,128)(2,1)}), bf16[3,1152,1152]{2,1,0:T(8,128)(2,1)}) %all-gather.9.cloned.1.call-update) | async-done | bytes 7962640 | tf_op jit(solution)/shard_map/all_gather | solution.py:104
  221.1 7.9 convolution_bitcast_fusion
  229.0 2.8 copy-done.12
  234.7 2.2 fusion.36
  237.6 3.7 fusion.37
  242.9 8.3 multiply_reduce_fusion.1
  251.2 8.7 fusion
  260.5 8.1 fusion.69
  268.6 2.4 fusion.84
  270.9 5.4 all-gather.15.cloned.1.call-done
  276.4 3.7 fusion.113
  283.8 2.1 fusion.85
  285.9 136.3 %all-gather.17.cloned.1.call-done = bf16[1152,4304]{1,0:T(8,128)(2,1)} async-done(((bf16[144,4304]{1,0:T(8,128)(2,1)}), bf16[1152,4304]{1,0:T(8,128)(2,1)}) %all-gather.17.cloned.1.call-update) | async-done | bytes 9916432 | tf_op jit(solution)/shard_map/all_gather | solution.py:135
  422.3 14.6 %fusion.114 = f32[512,4304]{0,1:T(8,128)} fusion(bf16[512,1152]{1,0:T(8,128)(2,1)} %copy-done.19, bf16[1152,4304]{1,0:T(8,128)(2,1)} %all-gather.17.cloned.1.call-done), kind=kOutput, calls=%fused_computation.180 | convolution fusion | flops 5077204992 | bytes 19910656 | tf_op jit(solution)/shard_map/dot_general | solution.py:15
  436.8 26.3 %all-gather.19.cloned.1.call-done = bf16[128,4304]{1,0:T(8,128)(2,1)} async-done(((bf16[16,4304]{1,0:T(8,128)(2,1)}), bf16[128,4304]{1,0:T(8,128)(2,1)}) %all-gather.19.cloned.1.call-update) | async-done | bytes 1101840 | tf_op jit(solution)/shard_map/all_gather | solution.py:92
  463.1 11.3 %fusion.9 = (bf16[512,4304]{0,1:T(8,128)(2,1)S(1)}, f32[512,4304]{0,1:T(8,128)}) fusion(f32[512,4304]{0,1:T(8,128)} %fusion.114, bf16[512,128]{1,0:T(8,128)(2,1)} %fusion.85, bf16[128,4304]{1,0:T(8,128)(2,1)} %all-gather.19.cloned.1.call-done), kind=kOutput, calls=%fused_computation.18 | convolution fusion | flops 586170368 | bytes 23269376 | tf_op jit(solution)/shard_map/dot_general | solution.py:15
  474.5 2.1 copy-done.21
  476.6 3.0 fusion.117
  479.7 129.8 %all-gather.21.cloned.1.call-done = bf16[4304,1152]{0,1:T(8,128)(2,1)} async-done(((bf16[4304,144]{0,1:T(8,128)(2,1)}), bf16[4304,1152]{0,1:T(8,128)(2,1)}) %all-gather.21.cloned.1.call-update) | async-done | bytes 9916432 | tf_op jit(solution)/shard_map/all_gather | solution.py:139
  609.5 14.9 %fusion.78 = f32[512,4304]{0,1:T(8,128)} fusion(bf16[4304,1152]{0,1:T(8,128)(2,1)} %all-gather.21.cloned.1.call-done, bf16[1,512,1152]{2,1,0:T(8,128)(2,1)} %param.16), kind=kOutput, calls=%fused_computation.117 | convolution fusion | flops 5077204992 | bytes 19910656 | tf_op jit(solution)/shard_map/dot_general | solution.py:19
  624.4 26.1 %all-gather.23.cloned.1.call-done = bf16[128,4304]{1,0:T(8,128)(2,1)} async-done(((bf16[16,4304]{1,0:T(8,128)(2,1)}), bf16[128,4304]{1,0:T(8,128)(2,1)}) %all-gather.23.cloned.1.call-update) | async-done | bytes 1101840 | tf_op jit(solution)/shard_map/all_gather | solution.py:90
  650.5 11.5 %fusion.16 = bf16[512,4304]{0,1:T(8,128)(2,1)S(1)} fusion(f32[512,4304]{0,1:T(8,128)} %get-tuple-element.19, f32[512,4304]{0,1:T(8,128)} %fusion.78, bf16[512,128]{1,0:T(8,128)(2,1)} %fusion.95, bf16[128,4304]{1,0:T(8,128)(2,1)} %all-gather.23.cloned.1.call-done), kind=kOutput, calls=%fused_computation.25 | convolution fusion | flops 608206848 | bytes 23269376 | tf_op jit(solution)/shard_map/dot_general | solution.py:15
  662.0 10.7 %fusion.116 = f32[512,1152]{1,0:T(8,128)S(1)} fusion(bf16[512,4304]{0,1:T(8,128)(2,1)S(1)} %fusion.16, bf16[1152,4304]{1,0:T(8,128)(2,1)} %all-gather.17.cloned.1.call-done), kind=kOutput, calls=%fused_computation.182 | convolution fusion | flops 5077204992 | bytes 16683008 | tf_op jit(solution)/shard_map/dot_general | solution.py:19
  681.6 2.4 fusion.38
  684.1 2.4 copy.40
  686.5 5.2 fusion.118
  691.7 14.8 %multiply_reduce_fusion = (f32[16,512]{1,0:T(8,128)}, f32[16,512,512]{1,2,0:T(8,128)}) fusion(f32[16,512,512]{1,2,0:T(8,128)} %get-tuple-element.15, f32[16,512]{1,0:T(8,128)} %log_add_fusion, bf16[512,16,72]{0,2,1:T(8,128)(2,1)} %bitcast.260, bf16[512,16,72]{0,2,1:T(8,128)(2,1)} %bitcast.270), kind=kOutput, calls=%fused_computation.1 | convolution fusion | flops 620748800 | bytes 35979264 | tf_op jit(solution)/shard_map/qhd,khd->hqk/dot_general | solution.py:167
  706.6 12.4 %multiply_convert_fusion = bf16[16,512,512]{1,2,0:T(8,128)(2,1)S(1)} fusion(f32[16,512,512]{1,2,0:T(8,128)} %get-tuple-element.22, f32[16,512,512]{1,2,0:T(8,128)} %get-tuple-element.15, f32[16,512]{1,0:T(8,128)} %get-tuple-element.21, f32[16,512]{1,0:T(8,128)} %log_add_fusion), kind=kLoop, calls=%fused_computation | loop fusion | flops 20971520 | bytes 42008576 | tf_op jit(solution)/shard_map/convert_element_type | solution.py:179
  722.2 2.6 multiply_convert_fusion.1
  726.6 7.8 fusion.70
  742.3 2.8 fusion.51
  745.1 2.9 fusion.50
  750.5 3.8 fusion.86
  756.2 2.7 copy.46
  758.9 2.4 copy.45
  761.3 2.4 copy.44
  763.7 9.4 fusion.32
  775.3 2.3 fusion.110
  777.7 10.3 %fusion.115 = f32[512,1152]{1,0:T(8,128)} fusion(bf16[512,4304]{0,1:T(8,128)(2,1)S(1)} %bitcast.276, bf16[4304,1152]{0,1:T(8,128)(2,1)} %all-gather.21.cloned.1.call-done), kind=kOutput, calls=%fused_computation.181 | convolution fusion | flops 5077204992 | bytes 16683008 | tf_op jit(solution)/shard_map/dot_general | solution.py:15
  789.6 2.4 reduce-scatter.11.cloned.1.call-done
  793.7 73.5 %reduce-scatter.5.cloned.1.call-done = f32[5,16,1152]{2,1,0:T(8,128)} async-done(((f32[5,128,1152]{2,1,0:T(8,128)}), f32[5,16,1152]{2,1,0:T(8,128)}) %reduce-scatter.5.cloned.1.call-update) | async-done | bytes 368656 | tf_op jit(solution)/shard_map/reduce_scatter | solution.py:221
  868.8 73.8 %reduce-scatter.9.cloned.1.call-done = f32[5,16,1152]{2,1,0:T(8,128)} async-done(((f32[5,128,1152]{2,1,0:T(8,128)}), f32[5,16,1152]{2,1,0:T(8,128)}) %reduce-scatter.9.cloned.1.call-update) | async-done | bytes 368656 | tf_op jit(solution)/shard_map/reduce_scatter | solution.py:223
  944.4 4.3 fusion.74
  948.7 2.4 fusion.46
  951.1 27.9 %all-reduce.3.cloned.1.call-done = (bf16[5,16,1152]{2,1,0:T(8,128)(2,1)}, bf16[16,4304]{1,0:T(8,128)(2,1)}, bf16[5,16,1152]{2,1,0:T(8,128)(2,1)}, bf16[16,4304]{1,0:T(8,128)(2,1)}) async-done(((bf16[5,16,1152]{2,1,0:T(8,128)(2,1)}, bf16[16,4304]{1,0:T(8,128)(2,1)}, bf16[5,16,1152]{2,1,0:T(8,128)(2,1)}, bf16[16,4304]{1,0:T(8,128)(2,1)}), (bf16[5,16,1152]{2,1,0:T(8,128)(2,1)}, bf16[16,4304]{1,0:T(8,128)(2,1)}, ...) | async-done | bytes 644112 | tf_op jit(solution)/shard_map/psum | solution.py:227
  (206 shorter events, 65.0 us)
Async XLA Ops:
  7.2 5.5 copy-start
  7.2 49.3 %all-gather.11.cloned.1.call-start = ((), (), s32[]{:S(2)}) async-start(), calls=%async_computation.5 | async-start | bytes 1658880 | tf_op jit(solution)/shard_map/all_gather | solution.py:89
  7.9 92.8 %all-gather.13.cloned.1.call-start = ((), (), s32[]{:S(2)}) async-start(), calls=%async_computation.6 | async-start | bytes 1658880 | tf_op jit(solution)/shard_map/all_gather | solution.py:91
  8.7 212.4 %all-gather.9.cloned.1.call-start = ((), (), s32[]{:S(2)}) async-start(), calls=%async_computation.4 | async-start | bytes 8957952 | tf_op jit(solution)/shard_map/all_gather | solution.py:104
  9.4 267.0 %all-gather.15.cloned.1.call-start = ((), (), s32[]{:S(2)}) async-start(), calls=%async_computation.7 | async-start | bytes 2985984 | tf_op jit(solution)/shard_map/all_gather | solution.py:129
  10.0 5.2 copy-start.49
  10.0 5.2 copy-start.54
  10.0 412.3 %all-gather.17.cloned.1.call-start = ((), (), s32[]{:S(2)}) async-start(), calls=%async_computation.8 | async-start | bytes 11280384 | tf_op jit(solution)/shard_map/all_gather | solution.py:135
  10.6 452.5 %all-gather.19.cloned.1.call-start = ((), (), s32[]{:S(2)}) async-start(), calls=%async_computation.9 | async-start | bytes 1253376 | tf_op jit(solution)/shard_map/all_gather | solution.py:92
  11.2 598.3 %all-gather.21.cloned.1.call-start = ((), (), s32[]{:S(2)}) async-start(), calls=%async_computation.10 | async-start | bytes 11280384 | tf_op jit(solution)/shard_map/all_gather | solution.py:139
  11.9 638.6 %all-gather.23.cloned.1.call-start = ((), (), s32[]{:S(2)}) async-start(), calls=%async_computation.11 | async-start | bytes 1253376 | tf_op jit(solution)/shard_map/all_gather | solution.py:90
  12.7 775.3 %reduce-scatter.7.cloned.1.call-start = ((), (), s32[]{:S(2)}) async-start(), calls=%async_computation.13 | async-start | bytes 2506752 | tf_op jit(solution)/shard_map/reduce_scatter | solution.py:222
  12.9 208.2 %copy-start.46 = (f32[512]{0:T(512)}, f32[512]{0:T(512)S(1)}, u32[]{:S(2)}) copy-start(f32[512]{0:T(512)S(1)} %broadcast_multiply_fusion.5) | copy-start | bytes 6148
  13.4 207.7 %copy-start.51 = (f32[512]{0:T(512)}, f32[512]{0:T(512)S(1)}, u32[]{:S(2)}) copy-start(f32[512]{0:T(512)S(1)} %add_rsqrt_fusion.1) | copy-start | bytes 6148
  15.7 85.0 %copy-start.14 = (bf16[1,512,1152]{2,1,0:T(8,128)(2,1)S(1)}, bf16[1,512,1152]{2,1,0:T(8,128)(2,1)}, u32[]{:S(2)}) copy-start(bf16[1,512,1152]{2,1,0:T(8,128)(2,1)} %param.16) | copy-start | bytes 3538948
  102.8 129.0 %copy-start.33 = (bf16[512,128]{1,0:T(8,128)(2,1)S(1)}, bf16[512,128]{1,0:T(8,128)(2,1)}, u32[]{:S(2)}) copy-start(bf16[512,128]{1,0:T(8,128)(2,1)} %fusion.81) | copy-start | bytes 393220
  237.6 5.3 copy-start.9
  242.9 8.3 copy-start.3
  251.2 9.3 copy-start.13
  260.5 8.1 copy-start.60
  268.6 7.8 copy-start.17
  463.1 13.5 %copy-start.41 = (bf16[512,128]{1,0:T(8,128)(2,1)S(1)}, bf16[512,128]{1,0:T(8,128)(2,1)}, u32[]{:S(2)}) copy-start(bf16[512,128]{1,0:T(8,128)(2,1)} %fusion.95) | copy-start | bytes 393220
  479.6 312.4 %reduce-scatter.11.cloned.1.call-start = ((), (), s32[]{:S(2)}) async-start(), calls=%async_computation.15 | async-start | bytes 2506752 | tf_op jit(solution)/shard_map/reduce_scatter | solution.py:224
  661.9 10.8 %copy-start.22 = (bf16[512,4304]{0,1:T(8,128)(2,1)}, bf16[512,4304]{0,1:T(8,128)(2,1)S(1)}, u32[]{:S(2)}) copy-start(bf16[512,4304]{0,1:T(8,128)(2,1)S(1)} %fusion.16) | copy-start | bytes 13221892
  661.9 10.8 %copy-start.56 = (bf16[128]{0:T(256)(128)(2,1)S(1)}, bf16[128]{0:T(256)(128)(2,1)}, u32[]{:S(2)}) copy-start(bf16[128]{0:T(256)(128)(2,1)} %fusion.105) | copy-start | bytes 772
  661.9 10.8 %copy-start.59 = (bf16[128,4304]{1,0:T(8,128)(2,1)S(1)}, bf16[128,4304]{1,0:T(8,128)(2,1)}, u32[]{:S(2)}) copy-start(bf16[128,4304]{1,0:T(8,128)(2,1)} %all-gather.19.cloned.1.call-done) | copy-start | bytes 3305476
  677.0 4.6 copy-start.1
  706.6 160.6 %reduce-scatter.5.cloned.1.call-start = ((), (), s32[]{:S(2)}) async-start(), calls=%async_computation.12 | async-start | bytes 3317760 | tf_op jit(solution)/shard_map/reduce_scatter | solution.py:221
  706.6 12.4 %copy-start.4 = (bf16[512,1152]{0,1:T(8,128)(2,1)S(1)}, bf16[512,1152]{0,1:T(8,128)(2,1)}, u32[]{:S(2)}) copy-start(bf16[512,1152]{0,1:T(8,128)(2,1)} %copy-done.3) | copy-start | bytes 3538948
  722.2 12.7 %copy-start.42 = (bf16[512,128]{1,0:T(8,128)(2,1)}, bf16[512,128]{1,0:T(8,128)(2,1)S(1)}, u32[]{:S(2)}) copy-start(bf16[512,128]{1,0:T(8,128)(2,1)S(1)} %fusion.92) | copy-start | bytes 393220
  722.2 4.2 copy-start.38
  726.5 10.0 %copy-start.44 = (bf16[512,128]{1,0:T(8,128)(2,1)}, bf16[512,128]{1,0:T(8,128)(2,1)S(1)}, u32[]{:S(2)}) copy-start(bf16[512,128]{1,0:T(8,128)(2,1)S(1)} %fusion.93) | copy-start | bytes 393220
  726.5 8.3 copy-start.47
  726.5 8.4 copy-start.50
  726.5 8.4 copy-start.52
  726.5 8.4 copy-start.55
  742.2 200.4 %reduce-scatter.9.cloned.1.call-start = ((), (), s32[]{:S(2)}) async-start(), calls=%async_computation.14 | async-start | bytes 3317760 | tf_op jit(solution)/shard_map/reduce_scatter | solution.py:223
  742.3 5.7 copy-start.8
  742.3 5.7 copy-start.34
  745.1 4.3 copy-start.2
  745.1 4.3 copy-start.32
  750.5 4.4 copy-start.16
  756.2 222.9 %all-reduce.3.cloned.1.call-start = ((), (), s32[]{:S(2)}) async-start(), calls=%async_computation.16 | async-start | bytes 1294336 | tf_op jit(solution)/shard_map/psum | solution.py:227
  763.7 9.4 copy-start.26
  763.7 9.5 copy-start.43
  773.1 4.6 slice-start
  944.4 4.3 copy-start.24
  944.4 4.3 copy-start.37
  (30 other events, 61.0 us)
Sparse Core Ops, SparseCore 0:
  10.2 46.1 all-gather.10
  58.7 41.9 all-gather.12
  103.0 118.0 all-gather.8
  223.1 53.1 all-gather.14
  278.4 143.8 all-gather.16
  424.3 38.7 all-gather.18
  465.3 144.1 all-gather.20
  611.6 38.7 all-gather.22
  653.9 67.0 reduce-scatter.6
  724.4 67.5 reduce-scatter.10
  795.6 71.4 reduce-scatter.4
  871.0 71.6 reduce-scatter.8
  945.8 33.1 all-reduce.2
where the time goes:
time: 996 us; the launch traced here: 992 us
  waiting for transfers between devices  704 us (71%)
  matrix products  205 us (21%)
  other arithmetic  43.1 us (4%)
  local copies, waits for them, and re-layouts  25 us (3%)
  between operations  15.6 us (2%)
    all_gather x1, waiting for transfers between devices, per_device(): lax.all_gather(mlp_first, 'shard', axis=0, tiled=True)  136 us
    all_gather x1, waiting for transfers between devices, per_device(): lax.all_gather(mlp_second, 'shard', axis=1, tiled=True)  130 us
    all_gather x1, waiting for transfers between devices, per_device(): lax.all_gather(qkv_weight, 'shard', axis=1, tiled=True)  118 us
    reduce_scatter x1, waiting for transfers between devices, per_device(): lax.psum_scatter(local_up_narrow, 'shard', scatter_dimension=1, tiled=True)  73.8 us
    reduce_scatter x1, waiting for transfers between devices, per_device(): lax.psum_scatter(local_down_narrow, 'shard', scatter_dimension=1, tiled=T...  73.5 us
    dot_general x15, matrix products, dot_plain(): return jnp.dot(left, right, preferred_element_type=jnp.float32)  70.5 us
    dot_general x15, matrix products, dot_last(): lax.dot_general(left, right, (((1,), (1,)), ((), ())), preferred_element_...  48.9 us
    all_gather x1, waiting for transfers between devices, per_device(): lax.all_gather(down_narrow, 'shard', axis=1, tiled=True)  40.8 us
  transfers between devices with their start and end apart: 13, of which 12 were waited for; matrix products, arithmetic and copies ran while one was open for 25% of the time, Pallas kernels for 0%

commit v1 on v0

--- a/solution.py
+++ b/solution.py
@@ -1,6 +1,8 @@
 import jax
 import jax.numpy as jnp
 from jax import lax
+from jax.experimental import pallas as pl
+from jax.experimental.pallas import tpu as pltpu
 from jax.sharding import PartitionSpec as P
 
 HEAD_DIM = 72
@@ -9,6 +11,126 @@
 
 GELU_SCALE = 0.7978845608028654
 GELU_CUBE = 0.044715
+
+
+MESH=pl.DeviceIdType.MESH
+CH=[(c*384,384) for c in range(5)]+[(1920,256)]
+class Net:
+    def __init__(self, loc, buf, ss, rs):
+        self.loc=loc; self.buf=buf; self.ss=ss; self.rs=rs
+        r=lax.axis_index("rep"); s=lax.axis_index("shard")
+        self.y=r//2; self.c=lax.rem(r,2); self.z=s//2; self.x=lax.rem(s,2)
+    def piece(self,g,ry,rc,z,x,own=False):
+        kind,i=g
+        s=2*z+x; q=2*ry+rc
+        N,A,M,W=self.loc if own else self.buf
+        if kind=='N': return N.at[pl.ds(3*q,3)] if own else N.at[pl.ds(3*q,3),pl.ds(pl.multiple_of(16*s,16),16)]
+        if kind=='A': return A.at[q,pl.ds(48*i,48)] if own else A.at[q,pl.ds(pl.multiple_of(144*s+48*i,16),48)]
+        if kind=='M':
+            o,w=CH[i]; cs=pl.ds(pl.multiple_of(ry*2176+o,128),w)
+            return M.at[rc,:,cs] if own else M.at[rc,pl.ds(pl.multiple_of(144*s,16),144),cs]
+        cs=pl.ds(pl.multiple_of(ry*2176,128),2176)
+        return W.at[rc,:,cs] if own else W.at[rc,pl.ds(pl.multiple_of(16*s,16),16),cs]
+    def dev(self,y=None,c=None,z=None,x=None):
+        y=self.y if y is None else y; c=self.c if c is None else c
+        z=self.z if z is None else z; x=self.x if x is None else x
+        return (2*y+c,2*z+x)
+    def cp(self,gi,slot,src,dst,dev):
+        return pltpu.make_async_remote_copy(src,dst,self.ss.at[gi,slot],self.rs.at[gi,slot],device_id=dev,device_id_type=MESH)
+    def Zc(self,gi,g,k):
+        p=self.piece(g,self.y,self.c,self.z,self.x)
+        return self.cp(gi,k-1,self.piece(g,self.y,self.c,self.z,self.x,True),p,self.dev(z=lax.rem(self.z+k,4)))
+    def src(self,k): return lax.rem(self.z+4-k,4)
+    def fwd(self,gi,g,slot,ry,z,x,dev,own=False):
+        p=self.piece(g,ry,self.c,z,x)
+        return self.cp(gi,slot,self.piece(g,ry,self.c,z,x,True) if own else p,p,dev)
+    def X(self,gi,g,k,own=False): return self.fwd(gi,g,3+k,self.y,self.src(k),self.x,self.dev(x=1-self.x),own)
+    def XD(self,gi,g): return self.fwd(gi,g,7,1-self.y,self.z,self.x,self.dev(x=1-self.x),True)
+    def Y(self,gi,g,k): return self.fwd(gi,g,7+k,self.y,self.src(k),self.x,self.dev(y=1-self.y))
+    def Dy(self,gi,g,k): return self.fwd(gi,g,10+k,self.y,self.src(k),1-self.x,self.dev(y=1-self.y))
+    def Dx(self,gi,g,k): return self.fwd(gi,g,10+k,1-self.y,self.src(k),self.x,self.dev(x=1-self.x))
+    def Cz(self,gi,g,k): return self.fwd(gi,g,13+k,self.y,self.src(k),self.x,self.dev(c=1-self.c))
+    def Cx(self,gi,g,k): return self.fwd(gi,g,17+k,self.y,self.src(k),1-self.x,self.dev(c=1-self.c))
+    def Cxd(self,gi,g): return self.fwd(gi,g,21,1-self.y,self.z,1-self.x,self.dev(c=1-self.c))
+    def Cy(self,gi,g,k): return self.fwd(gi,g,21+k,1-self.y,self.src(k),self.x,self.dev(c=1-self.c))
+    def Cd(self,gi,g,k): return self.fwd(gi,g,24+k,1-self.y,self.src(k),1-self.x,self.dev(c=1-self.c))
+    def nx(self,gi): return 1 if gi%2 else 0
+    def loop(self,lo,hi,f):
+        def body(k,_):
+            f(k); return 0
+        lax.fori_loop(lo,hi,body,0)
+    def A(self,gi,g):
+        self.loop(1,4,lambda k: self.Zc(gi,g,k).start())
+        self.X(gi,g,0,True).start(); self.XD(gi,g).start()
+    def B(self,gi,g):
+        def f(k):
+            self.Zc(gi,g,k).wait_recv()
+            self.X(gi,g,k).start(); self.Y(gi,g,k).start(); self.Cz(gi,g,k).start()
+        self.loop(1,4,f)
+    def C(self,gi,g):
+        n=self.nx(gi)
+        self.X(gi,g,0,True).wait_recv(); self.Cx(gi,g,0).start()
+        self.XD(gi,g).wait_recv(); self.Cxd(gi,g).start()
+        def f(k):
+            self.Y(gi,g,k).wait_recv(); self.Cy(gi,g,k).start()
+            self.X(gi,g,k).wait_recv(); self.Cx(gi,g,k).start()
+        def fx(k):
+            f(k); self.Dx(gi,g,k).start()
+        def fy(k):
+            f(k); self.Dy(gi,g,k).start()
+        if n: self.loop(1,1+n,fx)
+        self.loop(1+n,4,fy)
+    def D(self,gi,g):
+        def f(k):
+            self.Dy(gi,g,k).wait_recv(); self.Cd(gi,g,k).start()
+        self.loop(1,4,f)
+    def E(self,gi,g):
+        self.Cx(gi,g,0).wait_recv(); self.Cxd(gi,g).wait_recv()
+        def f(k):
+            self.Cz(gi,g,k).wait_recv(); self.Cx(gi,g,k).wait_recv(); self.Cy(gi,g,k).wait_recv(); self.Cd(gi,g,k).wait_recv()
+        self.loop(1,4,f)
+    def F(self,gi,g):
+        def f(k):
+            for h in (self.Zc,self.X,self.Y,self.Dy,self.Cz,self.Cx,self.Cy,self.Cd): h(gi,g,k).wait_send()
+        self.loop(1,4,f)
+        self.X(gi,g,0).wait_send(); self.XD(gi,g).wait_send(); self.Cx(gi,g,0).wait_send(); self.Cxd(gi,g).wait_send()
+    def barrier(self):
+        b=pltpu.get_barrier_semaphore()
+        for k in (1,2,3): pl.semaphore_signal(b,1,device_id=self.dev(z=lax.rem(self.z+k,4)),device_id_type=MESH)
+        pl.semaphore_signal(b,1,device_id=self.dev(x=1-self.x),device_id_type=MESH)
+        pl.semaphore_signal(b,1,device_id=self.dev(y=1-self.y),device_id_type=MESH)
+        pl.semaphore_signal(b,1,device_id=self.dev(c=1-self.c),device_id_type=MESH)
+        pl.semaphore_wait(b,6)
+GROUPS=[('N',0),('A',0),('A',1),('A',2),('W',0)]+[('M',c) for c in range(6)]
+def schedule(n):
+    out=[]
+    for t in range(n+4):
+        for st,lag in (('E',4),('D',3),('C',2),('B',1),('A',0)):
+            g=t-lag
+            if 0<=g<n: out.append((st,g))
+    return out
+def gather_kernel(nl,na,nm,nw,N,A,M,W,ss,rs,ls):
+    net=Net((nl,na,nm,nw),(N,A,M,W),ss,rs)
+    net.barrier()
+    s=2*net.z+net.x
+    l=[pltpu.make_async_copy(nl,N.at[:,pl.ds(pl.multiple_of(16*s,16),16)],ls.at[0]),
+       pltpu.make_async_copy(na,A.at[:,pl.ds(pl.multiple_of(144*s,16),144)],ls.at[1]),
+       pltpu.make_async_copy(nm,M.at[:,pl.ds(pl.multiple_of(144*s,16),144)],ls.at[2]),
+       pltpu.make_async_copy(nw,W.at[:,pl.ds(pl.multiple_of(16*s,16),16)],ls.at[3])]
+    for st,g in schedule(len(GROUPS)):
+        getattr(net,st)(g,GROUPS[g])
+        if st=='A' and g==1:
+            for q in l: q.start()
+    for q in l: q.wait()
+    for g in range(len(GROUPS)): net.F(g,GROUPS[g])
+def gather(nl,na,nm,nw):
+    n=len(GROUPS)
+    return pl.pallas_call(gather_kernel,
+      out_shape=(jax.ShapeDtypeStruct((12,128,1152),jnp.bfloat16),jax.ShapeDtypeStruct((4,1152,1152),jnp.bfloat16),
+        jax.ShapeDtypeStruct((2,1152,4352),jnp.bfloat16),jax.ShapeDtypeStruct((2,128,4352),jnp.bfloat16)),
+      in_specs=[pl.BlockSpec(memory_space=pl.ANY)]*4,out_specs=[pl.BlockSpec(memory_space=pl.ANY)]*4,
+      scratch_shapes=[pltpu.SemaphoreType.DMA((n,28)),pltpu.SemaphoreType.DMA((n,28)),pltpu.SemaphoreType.DMA((4,))],
+      compiler_params=pltpu.CompilerParams(collective_id=1,has_side_effects=True),name="gather")(nl,na,nm,nw)
 
 
 def dot_plain(left, right):
@@ -85,13 +207,27 @@
     seq_len, width = hidden_in.shape
     heads = width // HEAD_DIM
     scaling = HEAD_DIM ** (-0.5)
-    narrow_down, wide_down, narrow_up, wide_up = (
-        lax.all_gather(down_narrow, "shard", axis=1, tiled=True),
-        lax.all_gather(down_wide, "shard", axis=0, tiled=True),
-        lax.all_gather(up_narrow, "shard", axis=1, tiled=True),
-        lax.all_gather(up_wide, "shard", axis=0, tiled=True),
-    )
-    ranks = narrow_down.shape[1]
+    features = mlp_first.shape[1]
+    wide = ((0, 0), (0, 0), (0, -features % 256))
+    narrow_local = jnp.concatenate(
+        [down_narrow[:3], up_narrow[:3], down_narrow[3:], up_narrow[3:], down_narrow[:2]]
+    )
+    attention_local = jnp.concatenate([qkv_weight, out_weight[None]])
+    mlp_local = jnp.pad(jnp.stack([mlp_first, mlp_second.T]), wide)
+    wide_local = jnp.pad(jnp.stack([up_wide, down_wide]), wide)
+    locals_ = (narrow_local, attention_local, mlp_local, wide_local)
+    if (lax.axis_size("rep"), lax.axis_size("shard")) == (4, 8):
+        narrow, attention, mlp, wides = gather(*locals_)
+    else:
+        narrow, attention, mlp, wides = [
+            lax.all_gather(each, "shard", axis=1, tiled=True) for each in locals_
+        ]
+    narrow_down = [narrow[0], narrow[1], narrow[2], narrow[6], narrow[7]]
+    narrow_up = [narrow[3], narrow[4], narrow[5], narrow[8], narrow[9]]
+    wide_up, wide_down = wides[0, :, :features], wides[1, :, :features]
+    qkv_full, out_full = attention[:3], attention[3]
+    first_full, second_full = mlp[0, :, :features], mlp[1, :, :features]
+    ranks = narrow_down[0].shape[0]
     select = (lax.broadcasted_iota(jnp.int32, (1, ranks), 1) // RANK == adapter_ids[0, 0]).astype(
         jnp.float32
     )
@@ -101,7 +237,7 @@
     qkv_main = jnp.einsum(
         "tr,jre->jte",
         columns,
-        lax.all_gather(qkv_weight, "shard", axis=1, tiled=True),
+        qkv_full,
         preferred_element_type=jnp.float32,
     )
     inner_qkv = [adapter_in(normed, narrow_down[member], select) for member in range(3)]
@@ -126,27 +262,27 @@
     )
     attended = attended.reshape(seq_len, width).astype(jnp.bfloat16)
     columns = attended
-    out_main = dot_plain(columns, lax.all_gather(out_weight, "shard", axis=0, tiled=True))
+    out_main = dot_plain(columns, out_full)
     inner_out = adapter_in(attended, narrow_down[3], select)
     middle = hidden_in + (out_main + dot_plain(inner_out, narrow_up[3]))
     normal_two, inverse_two = layer_stats(middle)
     normed_two = (normal_two * gain_two + shift_two).astype(jnp.bfloat16)
     columns = normed_two
-    first_main = dot_plain(columns, lax.all_gather(mlp_first, "shard", axis=0, tiled=True))
+    first_main = dot_plain(columns, first_full)
     inner_one = adapter_in(normed_two, narrow_down[4], select)
     before = first_main + dot_plain(inner_one, wide_up)
     active = jax.nn.gelu(before, approximate=True).astype(jnp.bfloat16)
-    second_main = dot_plain(active, lax.all_gather(mlp_second, "shard", axis=1, tiled=True))
+    second_main = dot_last(active, second_full)
     inner_two = adapter_in(active, wide_down, select)
     output = (middle + (second_main + dot_plain(inner_two, narrow_up[4]))).astype(jnp.bfloat16)
     grad_after = cotangent[0]
     columns = grad_after
-    active_main = dot_last(columns, lax.all_gather(mlp_second, "shard", axis=1, tiled=True))
+    active_main = dot_plain(columns, second_full)
     back_two, grad_wide_down, grad_up_fc = adapter_back(
         grad_after, active, inner_two, wide_down, narrow_up[4], select
     )
     grad_before = ((active_main + back_two) * gelu_slope(before)).astype(jnp.bfloat16)
-    normed_two_main = dot_last(grad_before, lax.all_gather(mlp_first, "shard", axis=0, tiled=True))
+    normed_two_main = dot_last(grad_before, first_full)
     back_one, grad_down_fc, grad_wide_up = adapter_back(
         grad_before, normed_two, inner_one, narrow_down[4], wide_up, select
     )
@@ -154,7 +290,7 @@
         normed_two_main + back_one, normal_two, inverse_two, gain_two
     )
     grad_branch = grad_middle.astype(jnp.bfloat16)
-    attended_main = dot_last(grad_branch, lax.all_gather(out_weight, "shard", axis=0, tiled=True))
+    attended_main = dot_last(grad_branch, out_full)
     back_out, grad_down_out, grad_up_out = adapter_back(
         grad_branch, attended, inner_out, narrow_down[3], narrow_up[3], select
     )
@@ -195,7 +331,7 @@
     normed_main = jnp.einsum(
         "jte,jre->tr",
         grad_qkv,
-        lax.all_gather(qkv_weight, "shard", axis=1, tiled=True),
+        qkv_full,
         preferred_element_type=jnp.float32,
     )
     grad_downs = []
@@ -215,19 +351,21 @@
     input_grad = (grad_middle + norm_back(normed_main, normal_one, inverse_one, gain_one)).astype(
         jnp.bfloat16
     )
-    local_down_narrow = jnp.stack(grad_downs + [grad_down_out, grad_down_fc])
-    local_up_narrow = jnp.stack(grad_ups + [grad_up_out, grad_up_fc])
-    shares = (
-        lax.psum_scatter(local_down_narrow, "shard", scatter_dimension=1, tiled=True),
-        lax.psum_scatter(grad_wide_down, "shard", scatter_dimension=0, tiled=True),
-        lax.psum_scatter(local_up_narrow, "shard", scatter_dimension=1, tiled=True),
-        lax.psum_scatter(grad_wide_up, "shard", scatter_dimension=0, tiled=True),
-    )
+    parts = grad_downs + [grad_down_out, grad_down_fc] + grad_ups + [grad_up_out, grad_up_fc]
+    parts = parts + [grad_wide_down, grad_wide_up]
+    share = lax.psum_scatter(
+        jnp.concatenate(parts, axis=1).astype(jnp.bfloat16),
+        "shard",
+        scatter_dimension=0,
+        tiled=True,
+    )
+    total = lax.psum(share, "rep").astype(jnp.float32)
+    narrows = total[:, : 10 * width].reshape(-1, 10, width).transpose(1, 0, 2)
     totals = (
-        lax.psum(shares[0].astype(jnp.bfloat16), "rep").astype(jnp.float32),
-        lax.psum(shares[1].astype(jnp.bfloat16), "rep").astype(jnp.float32),
-        lax.psum(shares[2].astype(jnp.bfloat16), "rep").astype(jnp.float32),
-        lax.psum(shares[3].astype(jnp.bfloat16), "rep").astype(jnp.float32),
+        narrows[:5],
+        total[:, 10 * width : 10 * width + features],
+        narrows[5:],
+        total[:, 10 * width + features :],
     )
     return (output[None], input_grad[None], totals[0], totals[1], totals[2], totals[3])
 

time: 996 us -> 650 us (0.65)
  waiting for transfers between devices: 704 us -> 164 us
  Pallas kernels: 0 us -> 160 us
  local copies, waits for them, and re-layouts: 25 us -> 70.5 us
    all_gather x8 -> x0, waiting for transfers between devices: 521 us -> none  [the longest x1 136 us: per_device(): lax.all_gather(mlp_first, 'shard', axis=0, tiled=True)]
    pallas_call x0 -> x1, Pallas kernels: none -> 160 us  [gather(): pl.pallas_call(gather_kernel, out_shape=(jax.ShapeDtypeStruct((12, 128, 1...]
    reduce_scatter x4 -> x0, waiting for transfers between devices: 150 us -> none  [the longest x1 73.8 us: per_device(): lax.psum_scatter(local_up_narrow, 'shard', scatter_dimension=1, tiled=True)]
    psum x1, waiting for transfers between devices: 27.9 us -> 94.4 us  [per_device(): total = lax.psum(share, 'rep').astype(jnp.float32)]
    unnamed x13 -> x3, waiting for transfers between devices: 5.11 us -> 69.7 us
    another operation x0 -> x10, local copies, waits for them, and re-layouts: none -> 18.5 us
    unnamed x130 -> x142, local copies, waits for them, and re-layouts: 11.6 us -> 29.8 us
    convert_element_type x9 -> x0, other arithmetic: 13.8 us -> none  [the longest x1 1.68 us: per_device(): lax.psum(shares[0].astype(jnp.bfloat16), 'rep').astype(jnp.float32)]
  transfers between devices with their start and end apart: 13 -> 2, of which waited for: 12 -> 2; matrix products, arithmetic and copies ran while one was open for 25% -> 6% of each run, Pallas kernels for 0% -> 0%
where the time goes in v1:
time: 650 us; the launch traced here: 642 us
  matrix products  196 us (30%)
  waiting for transfers between devices  164 us (25%)
  Pallas kernels  160 us (25%)
  local copies, waits for them, and re-layouts  70.5 us (11%)
  other arithmetic  35.2 us (5%)
  between operations  16.3 us (3%)
    pallas_call x1, Pallas kernels, gather(): pl.pallas_call(gather_kernel, out_shape=(jax.ShapeDtypeStruct((12, 128, 1...  160 us
    psum x1, waiting for transfers between devices, per_device(): total = lax.psum(share, 'rep').astype(jnp.float32)  94.4 us
    unnamed x3, waiting for transfers between devices  69.7 us
    dot_general x15, matrix products, dot_plain(): return jnp.dot(left, right, preferred_element_type=jnp.float32)  67.4 us
    dot_general x15, matrix products, dot_last(): lax.dot_general(left, right, (((1,), (1,)), ((), ())), preferred_element_...  44.5 us
    unnamed x142, local copies, waits for them, and re-layouts  29.8 us
    dot_general x12, matrix products, dot_first(): lax.dot_general(left, right, (((0,), (0,)), ((), ())), preferred_element_...  26.1 us
    another operation x10, local copies, waits for them, and re-layouts  18.5 us
  transfers between devices with their start and end apart: 2, of which 2 were waited for; matrix products, arithmetic and copies ran while one was open for 6% of the time, Pallas kernels for 0%

profile of v1, /device:TPU:0, one launch (start us, length us, event | category | flops | bytes accessed | tf_op | source)
XLA Modules:
  0.0 641.6 jit_solution(11303539776706295817)
XLA Ops:
  16.5 159.7 %gather.1 = (bf16[12,128,1152]{2,1,0:T(8,128)(2,1)}, bf16[4,1152,1152]{2,1,0:T(8,128)(2,1)}, bf16[2,1152,4352]{2,1,0:T(8,128)(2,1)}, bf16[2,128,4352]{2,1,0:T(8,128)(2,1)}) custom-call(bf16[12,16,1152]{2,1,0:T(8,128)(2,1)} %copy-done.25, bf16[4,144,1152]{2,1,0:T(8,128)(2,1)} %pad_maximum_fusion.na, bf16[2,144,4352]{2,1,0:T(8,128)(2,1)} %fusion.70.nm, ...), custom_call_target="tpu_custom_call" | custom-call | tf_op jit(solution)/shard_map/gather/pallas_call | solution.py:128
  180.7 7.2 %convolution_bitcast_fusion = f32[3,512,1152]{1,2,0:T(8,128)S(1)} fusion(bf16[4,1152,1152]{2,1,0:T(8,128)(2,1)} %get-tuple-element.10, bf16[512,1152]{1,0:T(8,128)(2,1)S(1)} %fusion.72), kind=kOutput, calls=%fused_computation.50 | convolution fusion | flops 4076863488 | bytes 18874368 | tf_op jit(solution)/shard_map/tr,jre->jte/dot_general | solution.py:237
  192.8 8.2 %multiply_reduce_fusion.1 = (f32[16,512]{1,0:T(8,128)S(1)}, f32[16,512,512]{1,2,0:T(8,128)}) fusion(bf16[512,16,72]{0,2,1:T(8,128)(2,1)S(1)} %bitcast.262, bf16[512,16,72]{0,2,1:T(8,128)(2,1)S(1)} %bitcast.252), kind=kOutput, calls=%fused_computation.6 | convolution fusion | flops 612360192 | bytes 19169280 | tf_op jit(solution)/shard_map/qhd,khd->hqk/dot_general | solution.py:252
  201.1 8.6 %fusion = f32[16,512]{1,0:T(8,128)S(1)} fusion(f32[16,512,512]{1,2,0:T(8,128)} %get-tuple-element.41, f32[16,512]{1,0:T(8,128)S(1)} %get-tuple-element.40), kind=kLoop, calls=%fused_computation.5 | loop fusion | flops 12574720 | bytes 16842752 | tf_op jit(solution)/shard_map/reduce_sum | solution.py:257
  210.2 8.0 %fusion.85 = bf16[16,72,512]{2,1,0:T(8,128)(2,1)S(1)} fusion(bf16[512,16,72]{0,2,1:T(8,128)(2,1)S(1)} %bitcast.267, f32[16,512,512]{1,2,0:T(8,128)} %get-tuple-element.41, f32[16,512]{1,0:T(8,128)S(1)} %fusion, f32[16,512]{1,0:T(8,128)S(1)} %get-tuple-element.40), kind=kOutput, calls=%fused_computation.128 | convolution fusion | flops 621346816 | bytes 19202048 | tf_op jit(solution)/shard_map/hqk,khd->qhd/dot_general | solution.py:260
  219.8 3.6 fusion.68
  227.6 14.6 %fusion.8 = f32[512,4304]{0,1:T(8,128)} fusion(bf16[512,1152]{1,0:T(8,128)(2,1)S(1)} %add_convert_fusion, bf16[2,1152,4352]{2,1,0:T(8,128)(2,1)} %get-tuple-element.12), kind=kOutput, calls=%fused_computation.17 | convolution fusion | flops 5077204992 | bytes 20021248 | tf_op jit(solution)/shard_map/dot_general | solution.py:137
  242.2 12.5 %fusion.2 = f32[4304,512]{1,0:T(8,128)} fusion(bf16[2,1152,4352]{2,1,0:T(8,128)(2,1)} %get-tuple-element.12, bf16[1,512,1152]{2,1,0:T(8,128)(2,1)S(1)} %copy-done.7), kind=kOutput, calls=%fused_computation.11 | convolution fusion | flops 5077204992 | bytes 20021248 | tf_op jit(solution)/shard_map/dot_general | solution.py:137
  256.2 7.1 %fusion.21 = (bf16[512,4304]{0,1:T(8,128)(2,1)}, f32[512,4304]{0,1:T(8,128)}) fusion(f32[512,4304]{0,1:T(8,128)S(1)} %copy-done.57, bf16[512,128]{1,0:T(8,128)(2,1)S(1)} %fusion.100, bf16[2,128,4352]{2,1,0:T(8,128)(2,1)S(1)} %copy-done.55), kind=kOutput, calls=%fused_computation.30 | convolution fusion | flops 586170368 | bytes 23281664 | tf_op jit(solution)/shard_map/dot_general | solution.py:137
  263.3 10.0 %fusion.28 = bf16[512,4304]{0,1:T(8,128)(2,1)S(1)} fusion(f32[512,4304]{0,1:T(8,128)} %get-tuple-element.45, f32[4304,512]{1,0:T(8,128)} %fusion.2, bf16[128,512]{1,0:T(8,128)(2,1)S(1)} %fusion.110, bf16[2,128,4352]{2,1,0:T(8,128)(2,1)S(1)} %copy-done.55), kind=kOutput, calls=%fused_computation.37 | convolution fusion | flops 608206848 | bytes 23281664 | tf_op jit(solution)/shard_map/dot_general | solution.py:137
  275.3 9.5 %fusion.6 = f32[512,1152]{1,0:T(8,128)S(1)} fusion(bf16[512,4304]{0,1:T(8,128)(2,1)S(1)} %fusion.28, bf16[2,1152,4352]{2,1,0:T(8,128)(2,1)} %get-tuple-element.12), kind=kOutput, calls=%fused_computation.15 | convolution fusion | flops 5077204992 | bytes 16793600 | tf_op jit(solution)/shard_map/dot_general | solution.py:141
  285.9 2.0 fusion.172
  291.5 3.6 fusion.66
  296.4 2.4 fusion.57
  298.8 2.4 copy.77
  301.2 9.0 %fusion.86 = bf16[16,72,512]{2,1,0:T(8,128)(2,1)S(1)} fusion(bf16[512,16,72]{0,2,1:T(8,128)(2,1)} %bitcast.257, f32[16,512,512]{1,2,0:T(8,128)} %get-tuple-element.41, f32[16,512]{1,0:T(8,128)} %log_add_fusion), kind=kOutput, calls=%fused_computation.129 | convolution fusion | flops 617152512 | bytes 19169280 | tf_op jit(solution)/shard_map/hqk,qhd->khd/dot_general | solution.py:306
  310.3 2.5 fusion.109
  314.1 11.3 %multiply_reduce_fusion = (f32[16,512]{1,0:T(8,128)S(1)}, f32[16,512,512]{1,2,0:T(8,128)}) fusion(f32[16,512,512]{1,2,0:T(8,128)} %get-tuple-element.41, f32[16,512]{1,0:T(8,128)S(1)} %copy-done.38, bf16[512,16,72]{0,2,1:T(8,128)(2,1)S(1)} %bitcast.258, bf16[512,16,72]{0,2,1:T(8,128)(2,1)S(1)} %bitcast.268), kind=kOutput, calls=%fused_computation.1 | convolution fusion | flops 620748800 | bytes 35979264 | tf_op jit(solution)/shard_map/qhd,khd->hqk/dot_general | solution.py:303
  325.4 12.1 %multiply_convert_fusion = bf16[16,512,512]{1,2,0:T(8,128)(2,1)S(1)} fusion(f32[16,512,512]{1,2,0:T(8,128)} %get-tuple-element.48, f32[16,512,512]{1,2,0:T(8,128)} %get-tuple-element.41, f32[16,512]{1,0:T(8,128)S(1)} %get-tuple-element.47, f32[16,512]{1,0:T(8,128)S(1)} %copy-done.38), kind=kLoop, calls=%fused_computation | loop fusion | flops 20971520 | bytes 42008576 | tf_op jit(solution)/shard_map/convert_element_type | solution.py:315
  337.5 2.6 multiply_convert_fusion.1
  341.7 2.4 fusion.108
  345.4 2.1 fusion.107
  348.8 2.0 fusion.101
  350.8 1.9 copy.88
  352.7 2.4 convolution_convert_fusion.2
  360.6 1.9 copy.91
  362.5 2.4 convolution_convert_fusion.9
  366.8 1.9 copy.90
  370.5 2.4 convolution_convert_fusion.11
  372.9 2.4 convolution_convert_fusion.10
  390.5 4.6 fusion.37
  395.1 4.5 fusion.36
  399.6 8.0 %copy.105 = bf16[128,20128]{1,0:T(8,128)(2,1)} copy(bf16[128,20128]{0,1:T(8,128)(2,1)} %fusion.36) | data formatting | bytes 10305536
  407.8 2.6 copy.83
  410.4 2.4 copy.82
  412.8 2.4 copy.81
  415.2 9.7 %fusion.49 = f32[512,1152]{1,0:T(8,128)S(1)} fusion(bf16[4,1152,1152]{2,1,0:T(8,128)(2,1)} %get-tuple-element.10, bf16[1,512,1152]{2,1,0:T(8,128)(2,1)} %copy.83, bf16[1,512,1152]{2,1,0:T(8,128)(2,1)} %copy.82, bf16[1,512,1152]{2,1,0:T(8,128)(2,1)} %copy.81), kind=kOutput, calls=%fused_computation.76 | convolution fusion | flops 4080402432 | bytes 13860864 | tf_op jit(solution)/shard_map/jte,jre->tr/dot_general | solution.py:331
  428.1 3.3 fusion.171
  431.4 10.4 %fusion.4 = f32[512,1152]{1,0:T(8,128)} fusion(bf16[512,4304]{0,1:T(8,128)(2,1)S(1)} %bitcast.275, bf16[2,1152,4352]{2,1,0:T(8,128)(2,1)} %get-tuple-element.12), kind=kOutput, calls=%fused_computation.13 | convolution fusion | flops 5077204992 | bytes 16793600 | tf_op jit(solution)/shard_map/dot_general | solution.py:141
  441.8 69.7 %reduce-scatter.4.cloned.1.call-done = bf16[16,20128]{1,0:T(8,128)(2,1)} async-done(((bf16[128,20128]{1,0:T(8,128)(2,1)}), bf16[16,20128]{1,0:T(8,128)(2,1)}) %reduce-scatter.4.cloned.1.call-update) | async-done | bytes 644112
  511.5 4.8 copy.106
  516.4 4.3 fusion.90
  520.7 2.5 fusion.65
  523.2 94.4 %all-reduce.4.cloned.1.call-done = bf16[16,20128]{0,1:T(8,128)(2,1)} async-done(((bf16[16,20128]{0,1:T(8,128)(2,1)}), bf16[16,20128]{0,1:T(8,128)(2,1)}) %all-reduce.4.cloned.1.call-update) | async-done | bytes 644112 | tf_op jit(solution)/shard_map/psum | solution.py:362
  617.6 3.2 fusion.173
  620.8 2.9 copy.96
  625.1 4.1 slice.122
  629.2 4.2 copy.94
  (195 shorter events, 68.1 us)
Async XLA Ops:
  7.2 3.4 copy-start
  7.2 3.4 copy-start.46
  7.2 3.4 copy-start.52
  7.2 504.3 %reduce-scatter.4.cloned.1.call-start = ((), (), s32[]{:S(2)}) async-start(), calls=%async_computation.2 | async-start | bytes 5824512
  8.8 2.9 copy-start.48
  11.2 169.5 %copy-start.2 = (bf16[512,1152]{1,0:T(8,128)(2,1)}, bf16[512,1152]{1,0:T(8,128)(2,1)S(1)}, u32[]{:S(2)}) copy-start(bf16[512,1152]{1,0:T(8,128)(2,1)S(1)} %fusion.72) | copy-start | bytes 3538948
  11.7 3.1 copy-start.16
  11.8 3.1 copy-start.17
  177.6 10.3 %copy-start.33 = (bf16[512,128]{1,0:T(8,128)(2,1)}, bf16[512,128]{1,0:T(8,128)(2,1)S(1)}, u32[]{:S(2)}) copy-start(bf16[512,128]{1,0:T(8,128)(2,1)S(1)} %fusion.98) | copy-start | bytes 393220
  179.1 10.3 %copy-start.30 = (bf16[512,128]{1,0:T(8,128)(2,1)}, bf16[512,128]{1,0:T(8,128)(2,1)S(1)}, u32[]{:S(2)}) copy-start(bf16[512,128]{1,0:T(8,128)(2,1)S(1)} %fusion.97) | copy-start | bytes 393220
  180.6 10.5 %copy-start.36 = (bf16[512,128]{1,0:T(8,128)(2,1)}, bf16[512,128]{1,0:T(8,128)(2,1)S(1)}, u32[]{:S(2)}) copy-start(bf16[512,128]{1,0:T(8,128)(2,1)S(1)} %fusion.96) | copy-start | bytes 393220
  189.4 3.4 copy-start.3
  191.1 9.9 %copy-start.9 = (bf16[512,1152]{0,1:T(8,128)(2,1)}, bf16[512,1152]{0,1:T(8,128)(2,1)S(1)}, u32[]{:S(2)}) copy-start(bf16[512,1152]{0,1:T(8,128)(2,1)S(1)} %fusion.55) | copy-start | bytes 3538948
  192.8 17.4 %copy-start.13 = (bf16[512,1152]{0,1:T(8,128)(2,1)}, bf16[512,1152]{0,1:T(8,128)(2,1)S(1)}, u32[]{:S(2)}) copy-start(bf16[512,1152]{0,1:T(8,128)(2,1)S(1)} %fusion.54) | copy-start | bytes 3538948
  227.6 28.6 %copy-start.44 = (bf16[512,128]{1,0:T(8,128)(2,1)}, bf16[512,128]{1,0:T(8,128)(2,1)S(1)}, u32[]{:S(2)}) copy-start(bf16[512,128]{1,0:T(8,128)(2,1)S(1)} %fusion.100) | copy-start | bytes 393220
  227.6 14.6 %copy-start.7 = (bf16[1,512,1152]{2,1,0:T(8,128)(2,1)S(1)}, bf16[1,512,1152]{2,1,0:T(8,128)(2,1)}, u32[]{:S(2)}) copy-start(bf16[1,512,1152]{2,1,0:T(8,128)(2,1)} %param.16) | copy-start | bytes 3538948
  242.2 14.0 %copy-start.55 = (bf16[2,128,4352]{2,1,0:T(8,128)(2,1)S(1)}, bf16[2,128,4352]{2,1,0:T(8,128)(2,1)}, u32[]{:S(2)}) copy-start(bf16[2,128,4352]{2,1,0:T(8,128)(2,1)} %get-tuple-element.13) | copy-start | bytes 6684676
  242.2 14.0 %copy-start.57 = (f32[512,4304]{0,1:T(8,128)S(1)}, f32[512,4304]{0,1:T(8,128)}, u32[]{:S(2)}) copy-start(f32[512,4304]{0,1:T(8,128)} %fusion.8) | copy-start | bytes 26443780
  256.2 7.1 %copy-start.27 = (bf16[128,512]{1,0:T(8,128)(2,1)}, bf16[128,512]{1,0:T(8,128)(2,1)S(1)}, u32[]{:S(2)}) copy-start(bf16[128,512]{1,0:T(8,128)(2,1)S(1)} %fusion.110) | copy-start | bytes 393220
  288.7 2.8 copy-start.1
  301.2 11.6 %copy-start.37 = (bf16[512,128]{1,0:T(8,128)(2,1)S(1)}, bf16[512,128]{1,0:T(8,128)(2,1)}, u32[]{:S(2)}) copy-start(bf16[512,128]{1,0:T(8,128)(2,1)} %copy-done.36) | copy-start | bytes 393220
  310.2 15.1 %copy-start.8 = (bf16[16,72,512]{2,1,0:T(8,128)(2,1)}, bf16[16,72,512]{2,1,0:T(8,128)(2,1)S(1)}, u32[]{:S(2)}) copy-start(bf16[16,72,512]{2,1,0:T(8,128)(2,1)S(1)} %fusion.86) | copy-start | bytes 3538948
  310.3 3.8 copy-start.6
  310.3 3.8 copy-start.14
  310.3 3.8 copy-start.38
  325.4 12.1 %copy-start.10 = (bf16[512,1152]{0,1:T(8,128)(2,1)S(1)}, bf16[512,1152]{0,1:T(8,128)(2,1)}, u32[]{:S(2)}) copy-start(bf16[512,1152]{0,1:T(8,128)(2,1)} %copy-done.9) | copy-start | bytes 3538948
  337.5 2.7 copy-start.4
  337.5 11.3 %slice-start = ((s8[4407296]{0:T(1024)(128)(4,1)}), s8[4194304]{0:T(1024)(128)(4,1)S(1)}, s32[]{:S(2)}) async-start(s8[4407296]{0:T(1024)(128)(4,1)} %bitcast.272), calls=%async_computation.3 | async-start | bytes 8388608
  340.1 3.9 copy-start.11
  340.2 3.9 copy-start.34
  340.2 8.6 %slice-start.1 = ((s8[4407296]{0:T(1024)(128)(4,1)}), s8[212992]{0:T(1024)(128)(4,1)S(1)}, s32[]{:S(2)}) async-start(s8[4407296]{0:T(1024)(128)(4,1)} %bitcast.272), calls=%async_computation.4 | async-start | bytes 425984
  341.6 5.9 copy-start.5
  341.6 5.9 copy-start.31
  344.1 4.7 copy-start.56
  379.0 7.0 %copy-start.20 = (bf16[128,1152]{0,1:T(8,128)(2,1)S(1)}, bf16[128,1152]{0,1:T(8,128)(2,1)}, u32[]{:S(2)}) copy-start(bf16[128,1152]{0,1:T(8,128)(2,1)} %copy.88) | copy-start | bytes 884740
  379.0 7.7 %copy-start.23 = (bf16[128,1152]{0,1:T(8,128)(2,1)S(1)}, bf16[128,1152]{0,1:T(8,128)(2,1)}, u32[]{:S(2)}) copy-start(bf16[128,1152]{0,1:T(8,128)(2,1)} %copy.89) | copy-start | bytes 884740
  379.0 8.5 %copy-start.22 = (bf16[128,1152]{0,1:T(8,128)(2,1)S(1)}, bf16[128,1152]{0,1:T(8,128)(2,1)}, u32[]{:S(2)}) copy-start(bf16[128,1152]{0,1:T(8,128)(2,1)} %copy.90) | copy-start | bytes 884740
  379.0 9.2 %copy-start.21 = (bf16[128,1152]{0,1:T(8,128)(2,1)S(1)}, bf16[128,1152]{0,1:T(8,128)(2,1)}, u32[]{:S(2)}) copy-start(bf16[128,1152]{0,1:T(8,128)(2,1)} %copy.91) | copy-start | bytes 884740
  379.1 9.9 %copy-start.19 = (bf16[128,1152]{0,1:T(8,128)(2,1)S(1)}, bf16[128,1152]{0,1:T(8,128)(2,1)}, u32[]{:S(2)}) copy-start(bf16[128,1152]{0,1:T(8,128)(2,1)} %copy.92) | copy-start | bytes 884740
  380.9 8.8 %copy-start.18 = (bf16[128,1152]{0,1:T(8,128)(2,1)S(1)}, bf16[128,1152]{0,1:T(8,128)(2,1)}, u32[]{:S(2)}) copy-start(bf16[128,1152]{0,1:T(8,128)(2,1)} %copy.93) | copy-start | bytes 884740
  382.6 7.9 %copy-start.28 = (bf16[128,512]{1,0:T(8,128)(2,1)S(1)}, bf16[128,512]{1,0:T(8,128)(2,1)}, u32[]{:S(2)}) copy-start(bf16[128,512]{1,0:T(8,128)(2,1)} %copy-done.27) | copy-start | bytes 393220
  390.5 4.6 copy-start.45
  407.7 209.9 %all-reduce.4.cloned.1.call-start = ((), (), s32[]{:S(2)}) async-start(), calls=%async_computation.1 | async-start | bytes 10305536 | tf_op jit(solution)/shard_map/psum | solution.py:362
  415.2 9.8 %copy-start.35 = (bf16[512,128]{1,0:T(8,128)(2,1)S(1)}, bf16[512,128]{1,0:T(8,128)(2,1)}, u32[]{:S(2)}) copy-start(bf16[512,128]{1,0:T(8,128)(2,1)} %fusion.107) | copy-start | bytes 393220
  424.9 6.5 %slice-start.2 = ((s8[4407296]{0:T(1024)(128)(4,1)}), s8[4194304]{0:T(1024)(128)(4,1)S(1)}, s32[]{:S(2)}) async-start(s8[4407296]{0:T(1024)(128)(4,1)} %bitcast.274), calls=%async_computation.5 | async-start | bytes 8388608
  426.6 4.8 slice-start.3
  516.4 4.3 copy-start.15
  516.4 4.3 copy-start.26
  (16 other events, 27.8 us)
Sparse Core Ops, SparseCore 0:
  407.8 103.6 reduce-scatter.3
  516.5 101.0 all-reduce.3
